TPU v7x, 32 devices: a whole 2x2x4 slice. The times are simulated.
32 devices in a mesh: dp: 16 (over z, x, core), tensor: 2 (over y).
Axes of the slice: x: 2, y: 2, z: 4, core: 2. Of those that a mesh axis runs over, the one named last changes fastest.
Arguments:
- tokens: bfloat16 [8192, 640], P(('dp', 'tensor')), may hold values from -40 to 40
- cotangent: bfloat16 [8192, 640], P(('dp', 'tensor')), may hold values from -16 to 16
- positions: int32 [8192], P('dp'), may hold values from 0 to 1023, as said below
- w_query: bfloat16 [640, 1024], P('dp', 'tensor'), may hold values from -0.25 to 0.25
- w_key: bfloat16 [640, 256], P('dp'), may hold values from -0.25 to 0.25
- w_value: bfloat16 [640, 256], P('dp'), may hold values from -0.25 to 0.25
- w_out: bfloat16 [640, 1024], P('dp', 'tensor'), may hold values from -0.1875 to 0.1875
- w_gate: bfloat16 [640, 2048], P('dp', 'tensor'), may hold values from -0.25 to 0.25
- w_up: bfloat16 [640, 2048], P('dp', 'tensor'), may hold values from -0.25 to 0.25
- w_down: bfloat16 [640, 2048], P('dp', 'tensor'), may hold values from -0.125 to 0.125
- attn_in_gain: bfloat16 [640], replicated, may hold values from 0.25 to 1.75
- attn_out_gain: bfloat16 [640], replicated, may hold values from 0.25 to 1.75
- ffn_in_gain: bfloat16 [640], replicated, may hold values from 0.25 to 1.75
- ffn_out_gain: bfloat16 [640], replicated, may hold values from 0.25 to 1.75
- query_gain: bfloat16 [256], replicated, may hold values from 1 to 2
- key_gain: bfloat16 [256], replicated, may hold values from 1 to 2
Outputs:
- output: float32 [8192, 640], P(('dp', 'tensor'))
- input_grad: float32 [8192, 640], P(('dp', 'tensor'))
- grad_query: float32 [640, 1024], P('dp', 'tensor')
- grad_key: float32 [640, 256], P('dp')
- grad_value: float32 [640, 256], P('dp')
- grad_out: float32 [640, 1024], P('dp', 'tensor')
- grad_gate: float32 [640, 2048], P('dp', 'tensor')
- grad_up: float32 [640, 2048], P('dp', 'tensor')
- grad_down: float32 [640, 2048], P('dp', 'tensor')
- grad_attn_in_gain: float32 [640], replicated
- grad_attn_out_gain: float32 [640], replicated
- grad_ffn_in_gain: float32 [640], replicated
- grad_ffn_out_gain: float32 [640], replicated
- grad_query_gain: float32 [256], replicated
- grad_key_gain: float32 [256], replicated
Inputs may be any that keep to these rules, and one draw needn't show every extreme that they name: positions[t] is 0 where a document begins and positions[t - 1] + 1 elsewhere; a document begins at t = 0 and at every t with t % 1024 == 640; any other beginning lies at a t with t // 1024 odd and 640 < t % 1024 < 768.
All inputs are finite; a program needn't handle non-finite values.
Results may differ from a plain program's by a relative error of at most 0.018.
The roundings to bfloat16 on the way count: a program that leaves them out, or rounds other values in their place, can miss the bound.
Values may be sent and summed in bfloat16 or wider, within the bound.
No kernel may reach another device: no remote copies, remote signals or barrier semaphores. Data moves between devices by JAX's collectives and lax.ppermute only.
A program may use at most 128 MiB of HBM per device.

v0:
```python
import math
import jax
import jax.numpy as jnp
from jax import lax
from jax.sharding import PartitionSpec as P

HEAD_DIM = 256
WINDOW = 512
NORM_EPS = 1e-06
GELU_COEF = math.sqrt(2.0 / math.pi)


def shifted(value, axis, steps):
    count = lax.axis_size(axis)
    leading, last = (max(0, -steps), min(count, count - steps))
    return lax.ppermute(value, axis, [(source, source + steps) for source in range(leading, last)])


def norm_fwd(values, gain_vec):
    scale_inv = lax.rsqrt(jnp.mean(values * values, axis=-1, keepdims=True) + NORM_EPS)
    return (values * scale_inv * gain_vec, scale_inv)


def norm_bwd(values, scale_inv, gain_vec, upstream):
    scaled = upstream * gain_vec
    cube_inv = scale_inv * scale_inv * scale_inv
    inner_mean = jnp.mean(scaled * values, axis=-1, keepdims=True)
    return (scale_inv * scaled - values * cube_inv * inner_mean, upstream * values * scale_inv)


def rotary_tables(places):
    halfway = HEAD_DIM // 2
    frequency = jnp.exp(
        jnp.arange(halfway, dtype=jnp.float32) * (-2.0 * math.log(10000.0) / HEAD_DIM)
    )
    angles = places.astype(jnp.float32)[:, None] * frequency[None, :]
    return (jnp.cos(angles), jnp.sin(angles))


def rotate(inputs, cos_tab, sin_tab):
    halfway = inputs.shape[-1] // 2
    leading = inputs[..., :halfway]
    trailing = inputs[..., halfway:]
    return jnp.concatenate(
        [leading * cos_tab - trailing * sin_tab, trailing * cos_tab + leading * sin_tab], axis=-1
    )


def rotate_back(inputs, cos_tab, sin_tab):
    halfway = inputs.shape[-1] // 2
    leading = inputs[..., :halfway]
    trailing = inputs[..., halfway:]
    return jnp.concatenate(
        [leading * cos_tab + trailing * sin_tab, trailing * cos_tab - leading * sin_tab], axis=-1
    )


def gelu_parts(preact):
    inner_arg = GELU_COEF * (preact + 0.044715 * preact * preact * preact)
    tanh_val = jnp.tanh(inner_arg)
    gelu_val = 0.5 * preact * (1.0 + tanh_val)
    gelu_slope = 0.5 * (1.0 + tanh_val) + 0.5 * preact * (1.0 - tanh_val * tanh_val) * GELU_COEF * (
        1.0 + 3.0 * 0.044715 * preact * preact
    )
    return (gelu_val, gelu_slope)


def window_mask(places, window):
    query_idx = jnp.arange(window, dtype=jnp.int32)[:, None]
    key_idx = jnp.arange(2 * window, dtype=jnp.int32)[None, :]
    distance = query_idx + window - key_idx
    return (distance >= 0) & (distance < window) & (distance <= places[:, None])


def mul_plain(lhs_mat, rhs_mat):
    return jnp.dot(lhs_mat, rhs_mat, preferred_element_type=jnp.float32)


def mul_t(lhs_mat, rhs_mat):
    return lax.dot_general(
        lhs_mat, rhs_mat, (((1,), (1,)), ((), ())), preferred_element_type=jnp.float32
    )


def mul_tn(lhs_mat, rhs_mat):
    return lax.dot_general(
        lhs_mat, rhs_mat, (((0,), (0,)), ((), ())), preferred_element_type=jnp.float32
    )


def on_device(
    tokens,
    cotangent,
    positions,
    w_query,
    w_key,
    w_value,
    w_out,
    w_gate,
    w_up,
    w_down,
    attn_in_gain,
    attn_out_gain,
    ffn_in_gain,
    ffn_out_gain,
    query_gain,
    key_gain,
):
    own_rows = tokens.shape[0]
    group_rows = positions.shape[0]
    tensor_idx = lax.axis_index("tensor")
    score_scale = 1.0 / math.sqrt(HEAD_DIM)
    blocks = group_rows // WINDOW
    block_ids = jnp.arange(blocks, dtype=jnp.int32)
    gain_in = attn_in_gain.astype(jnp.float32)
    gain_pa = attn_out_gain.astype(jnp.float32)
    gain_pf = ffn_in_gain.astype(jnp.float32)
    gain_po = ffn_out_gain.astype(jnp.float32)
    gain_query = query_gain.astype(jnp.float32)
    gain_key = key_gain.astype(jnp.float32)

    def fetch_weights():
        return (
            lax.all_gather(w_query, "dp", axis=0, tiled=True),
            lax.all_gather(w_key, "dp", axis=0, tiled=True),
            lax.all_gather(w_value, "dp", axis=0, tiled=True),
            lax.all_gather(w_out, "dp", axis=0, tiled=True),
            lax.all_gather(w_gate, "dp", axis=0, tiled=True),
            lax.all_gather(w_up, "dp", axis=0, tiled=True),
            lax.all_gather(w_down, "dp", axis=0, tiled=True),
        )

    def reduce_grads(first_grad, second_grad, third_grad):
        return (
            lax.psum_scatter(first_grad, "dp", scatter_dimension=0, tiled=True),
            lax.psum_scatter(second_grad, "dp", scatter_dimension=0, tiled=True),
            lax.psum_scatter(third_grad, "dp", scatter_dimension=0, tiled=True),
        )

    def own_slice(whole, offset, row_count):
        return lax.dynamic_slice_in_dim(whole, offset, row_count, 0)

    front_weights = fetch_weights()
    full_query, full_key, full_value, full_out, full_gate, full_up, full_down = front_weights
    heads_local = full_query.shape[1] // HEAD_DIM
    inputs_f = tokens.astype(jnp.float32)
    normed_own, inv_in = norm_fwd(inputs_f, gain_in)
    normed_in = lax.all_gather(normed_own.astype(jnp.bfloat16), "tensor", axis=0, tiled=True)
    raw_query = mul_plain(normed_in, full_query).reshape(group_rows, heads_local, HEAD_DIM)
    raw_key = mul_plain(normed_in, full_key)
    raw_value = mul_plain(normed_in, full_value)
    unit_query, inv_query = norm_fwd(raw_query, gain_query)
    unit_key, inv_key = norm_fwd(raw_key, gain_key)
    cos_tab, sin_tab = rotary_tables(positions)
    rot_query = rotate(unit_query, cos_tab[:, None, :], sin_tab[:, None, :]).astype(jnp.bfloat16)
    rot_key = rotate(unit_key, cos_tab, sin_tab).astype(jnp.bfloat16)
    value_b = raw_value.astype(jnp.bfloat16)
    halo_key, halo_value = shifted((rot_key, value_b), "dp", 1)
    keys_ext = jnp.concatenate([halo_key, rot_key], axis=0)
    values_ext = jnp.concatenate([halo_value, value_b], axis=0)

    def block_scores(block_idx):
        offset = block_idx * WINDOW
        allowed = window_mask(positions, WINDOW)[None]
        scores = (
            jnp.einsum("qhd,kd->hqk", rot_query, keys_ext, preferred_element_type=jnp.float32)
            * score_scale
        )
        return (rot_query, keys_ext, values_ext, jnp.where(allowed, scores, -1e30), offset)

    def attend(unused, block_idx):
        queries, keys_blk, values_blk, masked, offset = block_scores(block_idx)
        row_max = jnp.max(masked, axis=-1, keepdims=True)
        weights_exp = jnp.exp(masked - row_max)
        row_sum = jnp.sum(weights_exp, axis=-1, keepdims=True)
        probs_b = (weights_exp / row_sum).astype(jnp.bfloat16)
        mixed_blk = jnp.einsum(
            "hqk,kd->qhd", probs_b, values_blk, preferred_element_type=jnp.float32
        ).astype(jnp.bfloat16)
        return (unused, (mixed_blk, (row_max + jnp.log(row_sum))[..., 0]))

    mixed_parts, lse_parts = lax.scan(attend, jnp.zeros((), jnp.float32), block_ids)[1]
    mixed_heads = mixed_parts.reshape(group_rows, heads_local, HEAD_DIM)
    attn_mixed = mixed_parts.reshape(group_rows, heads_local * HEAD_DIM)
    attn_proj = lax.psum_scatter(
        mul_t(own_slice(attn_mixed, jnp.int32(0), own_rows * lax.axis_size("tensor")), full_out),
        "tensor",
        scatter_dimension=0,
        tiled=True,
    )
    attn_norm, inv_pa = norm_fwd(attn_proj, gain_pa)
    residual = inputs_f + attn_norm
    ffn_in_f, inv_pf = norm_fwd(residual, gain_pf)
    normed_ffn = lax.all_gather(ffn_in_f.astype(jnp.bfloat16), "tensor", axis=0, tiled=True)
    gate_proj = mul_plain(normed_ffn, full_gate)
    up_proj = mul_plain(normed_ffn, full_up)
    gelu_val, gelu_slope = gelu_parts(gate_proj)
    hidden = (gelu_val * up_proj).astype(jnp.bfloat16)
    ffn_raw = lax.psum_scatter(
        mul_t(own_slice(hidden, jnp.int32(0), own_rows * lax.axis_size("tensor")), full_down),
        "tensor",
        scatter_dimension=0,
        tiled=True,
    )
    ffn_norm, inv_po = norm_fwd(ffn_raw, gain_po)
    output = residual + ffn_norm
    back_weights = fetch_weights()
    back_query, back_key, back_value, back_out, back_gate, back_up, back_down = back_weights
    upstream = cotangent.astype(jnp.float32)
    ffn_cot_f, po_terms = norm_bwd(ffn_raw, inv_po, gain_po, upstream)
    ffn_cot = lax.all_gather(ffn_cot_f.astype(jnp.bfloat16), "tensor", axis=0, tiled=True)
    grad_down = mul_tn(ffn_cot, hidden)
    hidden_cot = mul_plain(ffn_cot, back_down)
    gate_cot = (hidden_cot * up_proj * gelu_slope).astype(jnp.bfloat16)
    up_cot = (hidden_cot * gelu_val).astype(jnp.bfloat16)
    grad_gate = mul_tn(normed_ffn, gate_cot)
    grad_up = mul_tn(normed_ffn, up_cot)
    ffn_grads = (grad_gate, grad_up, grad_down)
    offset = jnp.int32(0)
    ffn_in_cot = lax.psum_scatter(
        mul_t(own_slice(gate_cot, offset, own_rows * lax.axis_size("tensor")), back_gate)
        + mul_t(own_slice(up_cot, offset, own_rows * lax.axis_size("tensor")), back_up),
        "tensor",
        scatter_dimension=0,
        tiled=True,
    )
    resid_back, pf_terms = norm_bwd(residual, inv_pf, gain_pf, ffn_in_cot)
    resid_cot = upstream + resid_back
    attn_cot_f, pa_terms = norm_bwd(attn_proj, inv_pa, gain_pa, resid_cot)
    attn_cot = lax.all_gather(attn_cot_f.astype(jnp.bfloat16), "tensor", axis=0, tiled=True)
    grad_out = mul_tn(attn_cot, attn_mixed)
    mixed_cot = (
        mul_plain(attn_cot, back_out)
        .astype(jnp.bfloat16)
        .reshape(group_rows, heads_local, HEAD_DIM)
    )

    def attend_back(carried, block_idx):
        key_ext_cot, value_ext_cot = carried
        queries, keys_blk, values_blk, masked, offset = block_scores(block_idx)
        lse_blk = lse_parts[block_idx]
        probs_f = jnp.exp(masked - lse_blk[..., None])
        delta_row = jnp.sum(
            mixed_cot.astype(jnp.float32) * mixed_heads.astype(jnp.float32), axis=-1
        )
        prob_cot = jnp.einsum(
            "qhd,kd->hqk", mixed_cot, values_blk, preferred_element_type=jnp.float32
        )
        score_cot = (probs_f * (prob_cot - jnp.transpose(delta_row)[:, :, None])).astype(
            jnp.bfloat16
        )
        query_cot = (
            jnp.einsum("hqk,kd->qhd", score_cot, keys_blk, preferred_element_type=jnp.float32)
            * score_scale
        )
        key_pair = (
            jnp.einsum("hqk,qhd->kd", score_cot, queries, preferred_element_type=jnp.float32)
            * score_scale
        )
        value_pair = jnp.einsum(
            "hqk,qhd->kd",
            probs_f.astype(jnp.bfloat16),
            mixed_cot,
            preferred_element_type=jnp.float32,
        )
        key_ext_cot = key_ext_cot + key_pair
        value_ext_cot = value_ext_cot + value_pair
        return ((key_ext_cot, value_ext_cot), query_cot)

    zero_ext = jnp.zeros((group_rows + WINDOW, HEAD_DIM), jnp.float32)
    ext_cots, query_parts = lax.scan(attend_back, (zero_ext, zero_ext), block_ids)
    key_ext_cot, value_ext_cot = ext_cots
    query_cot = query_parts.reshape(group_rows, heads_local, HEAD_DIM)
    back_key_cot, back_value_cot = shifted((key_ext_cot[:WINDOW], value_ext_cot[:WINDOW]), "dp", -1)
    own_key_cot = key_ext_cot[WINDOW:].at[group_rows - WINDOW :].add(back_key_cot)
    own_value_cot = value_ext_cot[WINDOW:].at[group_rows - WINDOW :].add(back_value_cot)
    key_cot, value_cot = lax.psum((own_key_cot, own_value_cot), "tensor")
    query_unit_cot = rotate_back(query_cot, cos_tab[:, None, :], sin_tab[:, None, :])
    query_raw_cot, qgain_terms = norm_bwd(raw_query, inv_query, gain_query, query_unit_cot)
    key_raw_cot, kgain_terms = norm_bwd(
        raw_key, inv_key, gain_key, rotate_back(key_cot, cos_tab, sin_tab)
    )
    query_proj_cot = query_raw_cot.reshape(group_rows, heads_local * HEAD_DIM).astype(jnp.bfloat16)
    keyval_cot = jnp.concatenate([key_raw_cot, value_cot], axis=1).astype(jnp.bfloat16)
    grad_query = mul_tn(normed_in, query_proj_cot)
    grad_keyval = mul_tn(normed_in, keyval_cot)
    attn_grads = reduce_grads(grad_query, grad_out, grad_keyval)
    ffn_done = reduce_grads(ffn_grads[0], ffn_grads[1], ffn_grads[2])
    in_query_cot = lax.psum_scatter(
        mul_t(
            own_slice(query_proj_cot, jnp.int32(0), own_rows * lax.axis_size("tensor")), back_query
        ),
        "tensor",
        scatter_dimension=0,
        tiled=True,
    )
    own_keyval = own_slice(keyval_cot, tensor_idx * own_rows, own_rows)
    in_cot = (
        in_query_cot
        + mul_t(own_keyval[:, :HEAD_DIM], back_key)
        + mul_t(own_keyval[:, HEAD_DIM:], back_value)
    )
    in_back, in_terms = norm_bwd(inputs_f, inv_in, gain_in, in_cot)
    input_grad = resid_cot + in_back
    own_kgain = own_slice(kgain_terms, tensor_idx * own_rows, own_rows)
    gain_totals = lax.psum(
        (
            jnp.sum(in_terms, axis=0),
            jnp.sum(pa_terms, axis=0),
            jnp.sum(pf_terms, axis=0),
            jnp.sum(po_terms, axis=0),
            jnp.sum(qgain_terms, axis=(0, 1)),
            jnp.sum(own_kgain, axis=0),
        ),
        ("dp", "tensor"),
    )
    red_query, red_out, red_keyval = attn_grads
    red_gate, red_up, red_down = ffn_done
    return (
        output,
        input_grad,
        red_query,
        red_keyval[:, :HEAD_DIM],
        red_keyval[:, HEAD_DIM:],
        red_out,
        red_gate,
        red_up,
        red_down,
        gain_totals[0],
        gain_totals[1],
        gain_totals[2],
        gain_totals[3],
        gain_totals[4],
        gain_totals[5],
    )


def solution(mesh):
    placed = (
        P(("dp", "tensor"), None),
        P(("dp", "tensor"), None),
        P("dp"),
        P("dp", "tensor"),
        P("dp", None),
        P("dp", None),
        P("dp", "tensor"),
        P("dp", "tensor"),
        P("dp", "tensor"),
        P("dp", "tensor"),
        P(),
        P(),
        P(),
        P(),
        P(),
        P(),
    )
    return jax.shard_map(
        on_device,
        mesh=mesh,
        in_specs=placed,
        out_specs=(
            P(("dp", "tensor"), None),
            P(("dp", "tensor"), None),
            P("dp", "tensor"),
            P("dp", None),
            P("dp", None),
            P("dp", "tensor"),
            P("dp", "tensor"),
            P("dp", "tensor"),
            P("dp", "tensor"),
            P(),
            P(),
            P(),
            P(),
            P(),
            P(),
        ),
        check_vma=False,
    )
```

profile of v0, /device:TPU:0, one launch (start us, length us, event | category | flops | bytes accessed | tf_op | source)
XLA Modules:
  0.0 803.0 jit_solution(5210754273820722378)
XLA Ops:
  10.5 24.2 %all_gather.41 = bf16[640,256]{1,0:T(8,128)(2,1)S(1)} all-gather(bf16[40,256]{1,0:T(8,128)(2,1)} %param.29), channel_id=1, replica_groups=mesh['dp'=16,'tensor'=2] {'dp'}, dimensions={0}, use_global_device_ids=true | all-gather | bytes 348160 | tf_op jit(solution)/shard_map/all_gather | solution.py:126
  35.9 10.6 %all_gather.40 = bf16[512,640]{1,0:T(8,128)(2,1)S(1)} all-gather(bf16[256,640]{1,0:T(8,128)(2,1)S(1)} %fusion.42), channel_id=1, replica_groups=mesh['dp'=16,'tensor'=2] {'tensor'}, dimensions={0}, use_global_device_ids=true | all-gather | bytes 983040 | tf_op jit(solution)/shard_map/all_gather | solution.py:148
  49.8 18.0 %all_gather.42 = bf16[640,256]{1,0:T(8,128)(2,1)S(1)} all-gather(bf16[40,256]{1,0:T(8,128)(2,1)S(1)} %copy-done.59), channel_id=1, replica_groups=mesh['dp'=16,'tensor'=2] {'dp'}, dimensions={0}, use_global_device_ids=true | all-gather | bytes 348160 | tf_op jit(solution)/shard_map/all_gather | solution.py:125
  71.0 3.0 collective-permute-start.1
  76.1 20.4 %all_gather.43 = bf16[640,512]{1,0:T(8,128)(2,1)S(1)} all-gather(bf16[40,512]{1,0:T(8,128)(2,1)S(1)} %copy-done.57), channel_id=1, replica_groups=mesh['dp'=16,'tensor'=2] {'dp'}, dimensions={0}, use_global_device_ids=true | all-gather | bytes 696320 | tf_op jit(solution)/shard_map/all_gather | solution.py:124
  96.5 21.2 %all_gather.44 = bf16[640,512]{1,0:T(8,128)(2,1)} all-gather(bf16[40,512]{1,0:T(8,128)(2,1)S(1)} %copy-done.58), channel_id=1, replica_groups=mesh['dp'=16,'tensor'=2] {'dp'}, dimensions={0}, use_global_device_ids=true | all-gather | bytes 696320 | tf_op jit(solution)/shard_map/all_gather | solution.py:127
  124.9 3.1 fusion.29
  132.4 19.5 %reduce-scatter.11.cloned.1.call-done = f32[256,640]{1,0:T(8,128)} async-done(((f32[512,640]{1,0:T(8,128)}), f32[256,640]{1,0:T(8,128)}) %reduce-scatter.11.cloned.1.call-update) | async-done | bytes 655376 | tf_op jit(solution)/shard_map/reduce_scatter | solution.py:185
  154.6 10.1 %all_gather.45 = bf16[512,640]{1,0:T(8,128)(2,1)S(1)} all-gather(bf16[256,640]{1,0:T(8,128)(2,1)S(1)} %multiply_convert_fusion.2), channel_id=1, replica_groups=mesh['dp'=16,'tensor'=2] {'tensor'}, dimensions={0}, use_global_device_ids=true | all-gather | bytes 983040 | tf_op jit(solution)/shard_map/all_gather | solution.py:194
  164.7 5.0 all-gather.4.cloned.1.call-done
  169.7 3.7 fusion.85
  173.4 36.2 %all-gather.6.cloned.1.call-done = bf16[640,1024]{1,0:T(8,128)(2,1)} async-done(((bf16[40,1024]{1,0:T(8,128)(2,1)}), bf16[640,1024]{1,0:T(8,128)(2,1)}) %all-gather.6.cloned.1.call-update) | async-done | bytes 1310736 | tf_op jit(solution)/shard_map/all_gather | solution.py:129
  209.6 4.9 multiply_convert_fusion.1
  214.5 34.9 %all-gather.8.cloned.1.call-done = bf16[640,1024]{1,0:T(8,128)(2,1)} async-done(((bf16[40,1024]{1,0:T(8,128)(2,1)}), bf16[640,1024]{1,0:T(8,128)(2,1)}) %all-gather.8.cloned.1.call-update) | async-done | bytes 1310736 | tf_op jit(solution)/shard_map/all_gather | solution.py:130
  249.4 3.7 fusion.86
  253.2 22.2 %reduce-scatter.13.cloned.1.call-done = f32[256,640]{1,0:T(8,128)} async-done(((f32[512,640]{1,0:T(8,128)}), f32[256,640]{1,0:T(8,128)}) %reduce-scatter.13.cloned.1.call-update) | async-done | bytes 655376 | tf_op jit(solution)/shard_map/reduce_scatter | solution.py:199
  280.4 9.9 %all_gather.49 = bf16[512,640]{1,0:T(8,128)(2,1)S(1)} all-gather(bf16[256,640]{1,0:T(8,128)(2,1)S(1)} %get-tuple-element.136), channel_id=1, replica_groups=mesh['dp'=16,'tensor'=2] {'tensor'}, dimensions={0}, use_global_device_ids=true | all-gather | bytes 983040 | tf_op jit(solution)/shard_map/all_gather | solution.py:211
  290.4 3.9 multiply_convert_fusion
  298.6 23.3 %reduce-scatter.15.cloned.1.call-done = f32[256,640]{1,0:T(8,128)} async-done(((f32[512,640]{1,0:T(8,128)}), f32[256,640]{1,0:T(8,128)}) %reduce-scatter.15.cloned.1.call-update) | async-done | bytes 655376 | tf_op jit(solution)/shard_map/reduce_scatter | solution.py:220
  325.2 10.1 %all_gather.50 = bf16[512,640]{1,0:T(8,128)(2,1)S(1)} all-gather(bf16[256,640]{1,0:T(8,128)(2,1)S(1)} %subtract_convert_fusion), channel_id=1, replica_groups=mesh['dp'=16,'tensor'=2] {'tensor'}, dimensions={0}, use_global_device_ids=true | all-gather | bytes 983040 | tf_op jit(solution)/shard_map/all_gather | solution.py:230
  336.0 2.8 fusion.1
  354.9 3.6 fusion.25
  359.8 7.9 collective-permute-done.3
  367.8 21.2 %all-reduce.5 = bf16[512,256]{0,1:T(8,128)(2,1)S(1)} all-reduce(f32[512,256]{0,1:T(8,128)S(1)} %slice_add_fusion), channel_id=1, replica_groups=mesh['dp'=16,'tensor'=2] {'tensor'}, use_global_device_ids=true, to_apply=%region_19.20 | all-reduce | flops 131072 | bytes 786432 | tf_op jit(solution)/shard_map/psum | solution.py:277
  394.7 3.6 fusion.93
  413.8 44.8 %all-reduce = (f32[640]{0:T(1024)}, f32[640]{0:T(1024)}, f32[640]{0:T(1024)}, f32[640]{0:T(1024)}, f32[256]{0:T(256)}, /*index=5*/f32[256]{0:T(256)}) all-reduce(f32[640]{0:T(1024)S(1)} %get-tuple-element.115, f32[640]{0:T(1024)S(1)} %get-tuple-element.111, ...), channel_id=1, replica_groups=mesh['dp'=16,'tensor'=2] {'dp','tensor'}, use_global_device_ids=true, to_apply=%region_28.29 | all-reduce | flops 3072 | bytes 24576 | tf_op jit(solution)/shard_map/psum | solution.py:306
  459.7 9.7 %reduce-scatter.21.cloned.1.call-done = f32[40,512]{1,0:T(8,128)} async-done(((f32[640,512]{1,0:T(8,128)}), f32[40,512]{1,0:T(8,128)}) %reduce-scatter.21.cloned.1.call-update) | async-done | bytes 81936 | tf_op jit(solution)/shard_map/reduce_scatter | solution.py:137
  470.8 66.1 %reduce-scatter.29.cloned.1.call-done = f32[40,1024]{1,0:T(8,128)} async-done(((f32[640,1024]{1,0:T(8,128)}), f32[40,1024]{1,0:T(8,128)}) %reduce-scatter.29.cloned.1.call-update) | async-done | bytes 163856 | tf_op jit(solution)/shard_map/reduce_scatter | solution.py:137
  536.9 67.6 %reduce-scatter.27.cloned.1.call-done = f32[40,1024]{1,0:T(8,128)} async-done(((f32[640,1024]{1,0:T(8,128)}), f32[40,1024]{1,0:T(8,128)}) %reduce-scatter.27.cloned.1.call-update) | async-done | bytes 163856 | tf_op jit(solution)/shard_map/reduce_scatter | solution.py:136
  604.5 67.6 %reduce-scatter.25.cloned.1.call-done = f32[40,1024]{1,0:T(8,128)} async-done(((f32[640,1024]{1,0:T(8,128)}), f32[40,1024]{1,0:T(8,128)}) %reduce-scatter.25.cloned.1.call-update) | async-done | bytes 163856 | tf_op jit(solution)/shard_map/reduce_scatter | solution.py:135
  672.1 61.7 %reduce-scatter.23.cloned.1.call-done = f32[40,512]{1,0:T(8,128)} async-done(((f32[640,512]{1,0:T(8,128)}), f32[40,512]{1,0:T(8,128)}) %reduce-scatter.23.cloned.1.call-update) | async-done | bytes 81936 | tf_op jit(solution)/shard_map/reduce_scatter | solution.py:136
  733.8 61.9 %reduce-scatter.19.cloned.1.call-done = f32[40,512]{1,0:T(8,128)} async-done(((f32[640,512]{1,0:T(8,128)}), f32[40,512]{1,0:T(8,128)}) %reduce-scatter.19.cloned.1.call-update) | async-done | bytes 81936 | tf_op jit(solution)/shard_map/reduce_scatter | solution.py:135
  (283 shorter events, 79.8 us)
Async XLA Ops:
  8.0 41.7 %copy-start.78 = (bf16[256]{0:T(256)(128)(2,1)S(1)}, bf16[256]{0:T(256)(128)(2,1)}, u32[]{:S(2)}) copy-start(bf16[256]{0:T(256)(128)(2,1)} %param.39) | copy-start | bytes 1540
  8.0 41.7 %copy-start.67 = (s32[512]{0:T(512)S(1)}, s32[512]{0:T(512)}, u32[]{:S(2)}) copy-start(s32[512]{0:T(512)} %param.26) | copy-start | bytes 6148
  8.0 41.8 %copy-start.59 = (bf16[40,256]{1,0:T(8,128)(2,1)S(1)}, bf16[40,256]{1,0:T(8,128)(2,1)}, u32[]{:S(2)}) copy-start(bf16[40,256]{1,0:T(8,128)(2,1)} %param.28) | copy-start | bytes 61444
  8.0 143.8 %reduce-scatter.11.cloned.1.call-start = ((), (), s32[]{:S(2)}) async-start(), calls=%async_computation.10 | async-start | bytes 1966080 | tf_op jit(solution)/shard_map/reduce_scatter | solution.py:185
  9.8 40.0 %copy-start.60 = (f32[256]{0:T(256)}, f32[256]{0:T(256)S(1)}, u32[]{:S(2)}) copy-start(f32[256]{0:T(256)S(1)} %get-tuple-element.151) | copy-start | bytes 3076
  47.6 77.3 %collective-permute-start = (bf16[512,256]{1,0:T(8,128)(2,1)}, bf16[512,256]{1,0:T(8,128)(2,1)}, u32[]{:S(2)}, u32[]{:S(2)}) collective-permute-start(bf16[512,256]{1,0:T(8,128)(2,1)} %convolution_convert_fusion.1), channel_id=1, source_target_pairs={{0,2},{2,4},{4,6},{6,8},{8,10},{10,12},{12,14},{14,16},{16,18},{18... | collective-permute-start | bytes 786440 | tf_op jit(solution)/shard_map/ppermute | solution.py:16
  68.9 27.6 %copy-start.58 = (bf16[40,512]{1,0:T(8,128)(2,1)S(1)}, bf16[40,512]{1,0:T(8,128)(2,1)}, u32[]{:S(2)}) copy-start(bf16[40,512]{1,0:T(8,128)(2,1)} %param.30) | copy-start | bytes 122884
  71.0 50.6 %collective-permute-start.1 = (bf16[512,256]{0,1:T(8,128)(2,1)}, bf16[512,256]{0,1:T(8,128)(2,1)}, u32[]{:S(2)}, u32[]{:S(2)}) collective-permute-start(bf16[512,256]{0,1:T(8,128)(2,1)} %pad_maximum_fusion.7), channel_id=1, source_target_pairs={{0,2},{2,4},{4,6},{6,8},{8,10},{10,12},{12,14},{14,16},{16,18},{18... | collective-permute-start | bytes 786440 | tf_op jit(solution)/shard_map/ppermute | solution.py:16
  75.2 45.4 %copy-start.33 = (f32[512,128]{1,0:T(8,128)}, f32[512,128]{1,0:T(8,128)S(1)}, u32[]{:S(2)}) copy-start(f32[512,128]{1,0:T(8,128)S(1)} %copy.49) | copy-start | bytes 786436
  96.5 22.5 %copy-start.8 = (bf16[640,512]{1,0:T(8,128)(2,1)}, bf16[640,512]{1,0:T(8,128)(2,1)S(1)}, u32[]{:S(2)}) copy-start(bf16[640,512]{1,0:T(8,128)(2,1)S(1)} %all_gather.43) | copy-start | bytes 1966084
  128.8 24.3 %copy-start.5 = (bf16[256,640]{1,0:T(8,128)(2,1)S(1)}, bf16[256,640]{1,0:T(8,128)(2,1)}, u32[]{:S(2)}) copy-start(bf16[256,640]{1,0:T(8,128)(2,1)} %param.24) | copy-start | bytes 983044
  130.5 39.2 %all-gather.4.cloned.1.call-start = ((), (), s32[]{:S(2)}) async-start(), calls=%async_computation.11 | async-start | bytes 1392640 | tf_op jit(solution)/shard_map/all_gather | solution.py:128
  131.1 78.5 %all-gather.6.cloned.1.call-start = ((), (), s32[]{:S(2)}) async-start(), calls=%async_computation.12 | async-start | bytes 1392640 | tf_op jit(solution)/shard_map/all_gather | solution.py:129
  131.7 117.7 %all-gather.8.cloned.1.call-start = ((), (), s32[]{:S(2)}) async-start(), calls=%async_computation.13 | async-start | bytes 1392640 | tf_op jit(solution)/shard_map/all_gather | solution.py:130
  132.3 143.2 %reduce-scatter.13.cloned.1.call-start = ((), (), s32[]{:S(2)}) async-start(), calls=%async_computation.14 | async-start | bytes 1966080 | tf_op jit(solution)/shard_map/reduce_scatter | solution.py:199
  253.2 68.8 %reduce-scatter.15.cloned.1.call-start = ((), (), s32[]{:S(2)}) async-start(), calls=%async_computation.15 | async-start | bytes 1966080 | tf_op jit(solution)/shard_map/reduce_scatter | solution.py:220
  298.5 24.7 %copy-start = (f32[256,640]{1,0:T(8,128)S(1)}, f32[256,640]{1,0:T(8,128)}, u32[]{:S(2)}) copy-start(f32[256,640]{1,0:T(8,128)} %reduce-scatter.11.cloned.1.call-done) | copy-start | bytes 1966084
  298.5 90.6 %all-reduce.4.cloned.1.call-start = ((), (), s32[]{:S(2)}) async-start(), calls=%async_computation.17 | async-start | bytes 1048576 | tf_op jit(solution)/shard_map/psum | solution.py:277
  339.7 4.6 collective-permute-start.2
  345.2 65.4 %reduce-scatter.17.cloned.1.call-start = ((), (), s32[]{:S(2)}) async-start(), calls=%async_computation.16 | async-start | bytes 1966080 | tf_op jit(solution)/shard_map/reduce_scatter | solution.py:289
  354.8 114.6 %reduce-scatter.21.cloned.1.call-start = ((), (), s32[]{:S(2)}) async-start(), calls=%async_computation.19 | async-start | bytes 1392640 | tf_op jit(solution)/shard_map/reduce_scatter | solution.py:137
  358.5 30.6 %copy-start.72 = (f32[128]{0:T(128)S(1)}, f32[128]{0:T(128)}, u32[]{:S(2)}) copy-start(f32[128]{0:T(128)} %copy-done.71) | copy-start | bytes 1540
  358.5 32.9 %copy-start.65 = (f32[256]{0:T(256)S(1)}, f32[256]{0:T(256)}, u32[]{:S(2)}) copy-start(f32[256]{0:T(256)} %copy-done.64) | copy-start | bytes 3076
  358.5 33.6 %copy-start.66 = (f32[512]{0:T(512)S(1)}, f32[512]{0:T(512)}, u32[]{:S(2)}) copy-start(f32[512]{0:T(512)} %get-tuple-element.148) | copy-start | bytes 6148
  358.5 9.2 %collective-permute-start.3 = (f32[512,256]{0,1:T(8,128)S(1)}, f32[512,256]{0,1:T(8,128)S(1)}, u32[]{:S(2)}, u32[]{:S(2)}) collective-permute-start(f32[512,256]{0,1:T(8,128)S(1)} %slice.103), channel_id=1, source_target_pairs={{2,0},{4,2},{6,4},{8,6},{10,8},{12,10},{14,12},{16,14},{18,16},{20... | collective-permute-start | bytes 1572872 | tf_op jit(solution)/shard_map/ppermute | solution.py:16
  394.6 142.3 %reduce-scatter.29.cloned.1.call-start = ((), (), s32[]{:S(2)}) async-start(), calls=%async_computation.23 | async-start | bytes 2785280 | tf_op jit(solution)/shard_map/reduce_scatter | solution.py:137
  398.3 206.3 %reduce-scatter.27.cloned.1.call-start = ((), (), s32[]{:S(2)}) async-start(), calls=%async_computation.22 | async-start | bytes 2785280 | tf_op jit(solution)/shard_map/reduce_scatter | solution.py:136
  401.9 270.2 %reduce-scatter.25.cloned.1.call-start = ((), (), s32[]{:S(2)}) async-start(), calls=%async_computation.21 | async-start | bytes 2785280 | tf_op jit(solution)/shard_map/reduce_scatter | solution.py:135
  405.5 328.3 %reduce-scatter.23.cloned.1.call-start = ((), (), s32[]{:S(2)}) async-start(), calls=%async_computation.20 | async-start | bytes 1392640 | tf_op jit(solution)/shard_map/reduce_scatter | solution.py:136
  408.4 387.3 %reduce-scatter.19.cloned.1.call-start = ((), (), s32[]{:S(2)}) async-start(), calls=%async_computation.18 | async-start | bytes 1392640 | tf_op jit(solution)/shard_map/reduce_scatter | solution.py:135
  410.5 48.1 %copy-start.7 = (f32[256,640]{1,0:T(8,128)S(1)}, f32[256,640]{1,0:T(8,128)}, u32[]{:S(2)}) copy-start(f32[256,640]{1,0:T(8,128)} %copy-done.6) | copy-start | bytes 1966084
  410.5 48.1 %copy-start.70 = (f32[256]{0:T(256)S(1)}, f32[256]{0:T(256)}, u32[]{:S(2)}) copy-start(f32[256]{0:T(256)} %get-tuple-element.150) | copy-start | bytes 3076
  (69 other events, 300.6 us)
Sparse Core Ops, SparseCore 0:
  130.7 21.1 reduce-scatter.10
  253.3 22.1 reduce-scatter.12
  298.6 23.2 reduce-scatter.14
  345.3 36.6 all-reduce.3
  384.1 22.8 reduce-scatter.16
  410.4 58.8 reduce-scatter.20
  473.7 63.1 reduce-scatter.28
  541.3 63.2 reduce-scatter.26
  608.9 63.2 reduce-scatter.24
  676.2 57.5 reduce-scatter.22
  738.0 57.6 reduce-scatter.18
Sparse Core Ops, SparseCore 1:
  133.3 36.4 all-gather.3
  171.9 37.7 all-gather.5
  211.8 37.6 all-gather.7
where the time goes:
time: 804 us; the launch traced here: 803 us
  waiting for transfers between devices  485 us (60%)
  blocking collectives  191 us (24%)
  matrix products  56 us (7%)
  other arithmetic  31.9 us (4%)
  between operations  16.8 us (2%)
  local copies, waits for them, and re-layouts  13.7 us (2%)
  starting transfers between devices  8.57 us (1%)
    reduce_scatter x2, waiting for transfers between devices, reduce_grads(): lax.psum_scatter(first_grad, 'dp', scatter_dimension=0, tiled=True)  129 us
    reduce_scatter x2, waiting for transfers between devices, reduce_grads(): lax.psum_scatter(second_grad, 'dp', scatter_dimension=0, tiled=True)  129 us
    reduce_scatter x2, waiting for transfers between devices, reduce_grads(): lax.psum_scatter(third_grad, 'dp', scatter_dimension=0, tiled=True)  75.8 us
    psum x1, blocking collectives, on_device(): lax.psum((jnp.sum(in_terms, axis=0), jnp.sum(pa_terms, axis=0), jnp.sum(p...  44.8 us
    all_gather x1, waiting for transfers between devices, fetch_weights(): lax.all_gather(w_up, 'dp', axis=0, tiled=True)  36.2 us
    all_gather x1, waiting for transfers between devices, fetch_weights(): lax.all_gather(w_down, 'dp', axis=0, tiled=True)  34.9 us
    all_gather x1, blocking collectives, fetch_weights(): lax.all_gather(w_value, 'dp', axis=0, tiled=True)  24.2 us
    reduce_scatter x1, waiting for transfers between devices, on_device(): lax.psum_scatter(mul_t(own_slice(gate_cot, offset, own_rows * lax.axis_si...  23.3 us
  transfers between devices with their start and end apart: 18, of which 13 were waited for; matrix products, arithmetic and copies ran while one was open for 7% of the time, Pallas kernels for 0%

commit v1 on v0

--- a/solution.py
+++ b/solution.py
@@ -8,6 +8,32 @@
 WINDOW = 512
 NORM_EPS = 1e-06
 GELU_COEF = math.sqrt(2.0 / math.pi)
+
+
+def grid_expand(local_x, array_dim):
+    local_x = jnp.moveaxis(local_x, 0, array_dim)
+    tmp = local_x.shape
+    return local_x.reshape(
+        *tmp[:array_dim], tmp[array_dim] * tmp[array_dim + 1], *tmp[array_dim + 2 :]
+    )
+
+
+def search_bands_now(point, mesh_dim):
+    mat_out, arr_next = (lax.axis_size(mesh_dim), lax.axis_index(mesh_dim))
+    res, part_next = (point[None], 1)
+    while part_next < mat_out:
+        nodes = []
+        no = 0
+        while no < mat_out:
+            nodes.append((no, no ^ part_next))
+            no += 1
+        next_value = lax.ppermute(res, axis_name=mesh_dim, perm=nodes)
+        current_arr = arr_next & part_next == 0
+        res = jnp.concatenate(
+            [jnp.where(current_arr, res, next_value), jnp.where(current_arr, next_value, res)]
+        )
+        part_next *= 2
+    return res
 
 
 def shifted(value, axis, steps):
@@ -120,8 +146,12 @@
     gain_key = key_gain.astype(jnp.float32)
 
     def fetch_weights():
+
+        def drive_the_loops(content, local_block, on_dim):
+            return grid_expand(search_bands_now(content, local_block), on_dim)
+
         return (
-            lax.all_gather(w_query, "dp", axis=0, tiled=True),
+            drive_the_loops(w_query, "dp", 0),
             lax.all_gather(w_key, "dp", axis=0, tiled=True),
             lax.all_gather(w_value, "dp", axis=0, tiled=True),
             lax.all_gather(w_out, "dp", axis=0, tiled=True),

time: 804 us -> 801 us (level)
  blocking collectives: 191 us -> 175 us
  waiting for transfers between devices: 485 us -> 495 us
    all_gather x1 -> x0, blocking collectives: 20.4 us -> none  [fetch_weights(): lax.all_gather(w_query, 'dp', axis=0, tiled=True)]
  transfers between devices with their start and end apart: 18 -> 22, of which waited for: 13 -> 16; matrix products, arithmetic and copies ran while one was open for 7% -> 8% of each run, Pallas kernels for 0% -> 0%
where the time goes in v1:
time: 801 us; the launch traced here: 800 us
  waiting for transfers between devices  495 us (62%)
  blocking collectives  175 us (22%)
  matrix products  53.8 us (7%)
  other arithmetic  35.1 us (4%)
  between operations  16.8 us (2%)
  local copies, waits for them, and re-layouts  13.5 us (2%)
  starting transfers between devices  10.7 us (1%)
    reduce_scatter x2, waiting for transfers between devices, reduce_grads(): lax.psum_scatter(first_grad, 'dp', scatter_dimension=0, tiled=True)  129 us
    reduce_scatter x2, waiting for transfers between devices, reduce_grads(): lax.psum_scatter(second_grad, 'dp', scatter_dimension=0, tiled=True)  129 us
    reduce_scatter x2, waiting for transfers between devices, reduce_grads(): lax.psum_scatter(third_grad, 'dp', scatter_dimension=0, tiled=True)  79.5 us
    psum x1, blocking collectives, on_device(): lax.psum((jnp.sum(in_terms, axis=0), jnp.sum(pa_terms, axis=0), jnp.sum(p...  45.7 us
    all_gather x1, waiting for transfers between devices, fetch_weights(): lax.all_gather(w_up, 'dp', axis=0, tiled=True)  36.1 us
    all_gather x1, waiting for transfers between devices, fetch_weights(): lax.all_gather(w_down, 'dp', axis=0, tiled=True)  34.9 us
    all_gather x1, blocking collectives, fetch_weights(): lax.all_gather(w_out, 'dp', axis=0, tiled=True)  25.3 us
    all_gather x1, blocking collectives, fetch_weights(): lax.all_gather(w_value, 'dp', axis=0, tiled=True)  23.7 us
  transfers between devices with their start and end apart: 22, of which 16 were waited for; matrix products, arithmetic and copies ran while one was open for 8% of the time, Pallas kernels for 0%

profile of v1, /device:TPU:0, one launch (start us, length us, event | category | flops | bytes accessed | tf_op | source)
XLA Modules:
  0.0 799.8 jit_solution(13552600891495246802)
XLA Ops:
  11.0 23.7 %all_gather.37 = bf16[640,256]{1,0:T(8,128)(2,1)S(1)} all-gather(bf16[40,256]{1,0:T(8,128)(2,1)} %param.29), channel_id=1, replica_groups=mesh['dp'=16,'tensor'=2] {'dp'}, dimensions={0}, use_global_device_ids=true | all-gather | bytes 348160 | tf_op jit(solution)/shard_map/all_gather | solution.py:156
  36.0 10.6 %all_gather.36 = bf16[512,640]{1,0:T(8,128)(2,1)S(1)} all-gather(bf16[256,640]{1,0:T(8,128)(2,1)S(1)} %fusion.39), channel_id=1, replica_groups=mesh['dp'=16,'tensor'=2] {'tensor'}, dimensions={0}, use_global_device_ids=true | all-gather | bytes 983040 | tf_op jit(solution)/shard_map/all_gather | solution.py:178
  49.8 18.0 %all_gather.38 = bf16[640,256]{1,0:T(8,128)(2,1)S(1)} all-gather(bf16[40,256]{1,0:T(8,128)(2,1)S(1)} %copy-done.58), channel_id=1, replica_groups=mesh['dp'=16,'tensor'=2] {'dp'}, dimensions={0}, use_global_device_ids=true | all-gather | bytes 348160 | tf_op jit(solution)/shard_map/all_gather | solution.py:155
  78.5 2.8 collective-permute-done.4
  82.9 25.3 %all_gather.39 = bf16[640,512]{1,0:T(8,128)(2,1)S(1)} all-gather(bf16[40,512]{1,0:T(8,128)(2,1)S(1)} %copy-done.55), channel_id=1, replica_groups=mesh['dp'=16,'tensor'=2] {'dp'}, dimensions={0}, use_global_device_ids=true | all-gather | bytes 696320 | tf_op jit(solution)/shard_map/all_gather | solution.py:157
  115.6 2.6 fusion.29
  122.6 23.3 %reduce-scatter.11.cloned.1.call-done = f32[256,640]{1,0:T(8,128)} async-done(((f32[512,640]{1,0:T(8,128)}), f32[256,640]{1,0:T(8,128)}) %reduce-scatter.11.cloned.1.call-update) | async-done | bytes 655376 | tf_op jit(solution)/shard_map/reduce_scatter | solution.py:215
  150.3 10.1 %all_gather.40 = bf16[512,640]{1,0:T(8,128)(2,1)S(1)} all-gather(bf16[256,640]{1,0:T(8,128)(2,1)S(1)} %multiply_convert_fusion.2), channel_id=1, replica_groups=mesh['dp'=16,'tensor'=2] {'tensor'}, dimensions={0}, use_global_device_ids=true | all-gather | bytes 983040 | tf_op jit(solution)/shard_map/all_gather | solution.py:224
  160.5 3.4 all-gather.4.cloned.1.call-done
  163.8 3.7 fusion.84
  167.5 36.1 %all-gather.6.cloned.1.call-done = bf16[640,1024]{1,0:T(8,128)(2,1)} async-done(((bf16[40,1024]{1,0:T(8,128)(2,1)}), bf16[640,1024]{1,0:T(8,128)(2,1)}) %all-gather.6.cloned.1.call-update) | async-done | bytes 1310736 | tf_op jit(solution)/shard_map/all_gather | solution.py:159
  203.6 4.9 multiply_convert_fusion.1
  208.5 34.9 %all-gather.8.cloned.1.call-done = bf16[640,1024]{1,0:T(8,128)(2,1)} async-done(((bf16[40,1024]{1,0:T(8,128)(2,1)}), bf16[640,1024]{1,0:T(8,128)(2,1)}) %all-gather.8.cloned.1.call-update) | async-done | bytes 1310736 | tf_op jit(solution)/shard_map/all_gather | solution.py:160
  243.4 3.7 fusion.85
  248.5 21.0 %reduce-scatter.13.cloned.1.call-done = f32[256,640]{1,0:T(8,128)} async-done(((f32[512,640]{1,0:T(8,128)}), f32[256,640]{1,0:T(8,128)}) %reduce-scatter.13.cloned.1.call-update) | async-done | bytes 655376 | tf_op jit(solution)/shard_map/reduce_scatter | solution.py:229
  275.0 9.9 %all_gather.44 = bf16[512,640]{1,0:T(8,128)(2,1)S(1)} all-gather(bf16[256,640]{1,0:T(8,128)(2,1)S(1)} %get-tuple-element.134), channel_id=1, replica_groups=mesh['dp'=16,'tensor'=2] {'tensor'}, dimensions={0}, use_global_device_ids=true | all-gather | bytes 983040 | tf_op jit(solution)/shard_map/all_gather | solution.py:241
  285.0 3.9 multiply_convert_fusion
  294.5 22.1 %reduce-scatter.15.cloned.1.call-done = f32[256,640]{1,0:T(8,128)} async-done(((f32[512,640]{1,0:T(8,128)}), f32[256,640]{1,0:T(8,128)}) %reduce-scatter.15.cloned.1.call-update) | async-done | bytes 655376 | tf_op jit(solution)/shard_map/reduce_scatter | solution.py:250
  321.3 10.1 %all_gather.45 = bf16[512,640]{1,0:T(8,128)(2,1)S(1)} all-gather(bf16[256,640]{1,0:T(8,128)(2,1)S(1)} %subtract_convert_fusion.1), channel_id=1, replica_groups=mesh['dp'=16,'tensor'=2] {'tensor'}, dimensions={0}, use_global_device_ids=true | all-gather | bytes 983040 | tf_op jit(solution)/shard_map/all_gather | solution.py:260
  332.2 2.7 fusion.1
  345.8 3.6 fusion.25
  350.8 7.9 collective-permute-done.7
  358.8 21.1 %all-reduce.5 = bf16[512,256]{0,1:T(8,128)(2,1)S(1)} all-reduce(f32[512,256]{0,1:T(8,128)S(1)} %slice_add_fusion), channel_id=1, replica_groups=mesh['dp'=16,'tensor'=2] {'tensor'}, use_global_device_ids=true, to_apply=%region_19.20 | all-reduce | flops 131072 | bytes 786432 | tf_op jit(solution)/shard_map/psum | solution.py:307
  384.8 3.6 fusion.92
  401.3 2.9 reduce-scatter.17.cloned.1.call-done
  406.2 45.7 %all-reduce = (f32[640]{0:T(1024)}, f32[640]{0:T(1024)}, f32[640]{0:T(1024)}, f32[640]{0:T(1024)}, f32[256]{0:T(256)}, /*index=5*/f32[256]{0:T(256)}) all-reduce(f32[640]{0:T(1024)S(1)} %get-tuple-element.117, f32[640]{0:T(1024)S(1)} %copy-done.69, f32[640]{0:T(1024)S(1)} %copy-done.68, ...), channel_id=1, replica_groups=mesh['dp'=16,'tensor'=2] {'dp','tensor'}, use_global_device_ids=true, to_apply=%region_28.29 | all-reduce | flops 3072 | bytes 24576 | tf_op jit(solution)/shard_map/psum | solution.py:336
  452.9 13.3 %reduce-scatter.21.cloned.1.call-done = f32[40,512]{1,0:T(8,128)} async-done(((f32[640,512]{1,0:T(8,128)}), f32[40,512]{1,0:T(8,128)}) %reduce-scatter.21.cloned.1.call-update) | async-done | bytes 81936 | tf_op jit(solution)/shard_map/reduce_scatter | solution.py:167
  467.7 66.2 %reduce-scatter.29.cloned.1.call-done = f32[40,1024]{1,0:T(8,128)} async-done(((f32[640,1024]{1,0:T(8,128)}), f32[40,1024]{1,0:T(8,128)}) %reduce-scatter.29.cloned.1.call-update) | async-done | bytes 163856 | tf_op jit(solution)/shard_map/reduce_scatter | solution.py:167
  533.9 67.6 %reduce-scatter.27.cloned.1.call-done = f32[40,1024]{1,0:T(8,128)} async-done(((f32[640,1024]{1,0:T(8,128)}), f32[40,1024]{1,0:T(8,128)}) %reduce-scatter.27.cloned.1.call-update) | async-done | bytes 163856 | tf_op jit(solution)/shard_map/reduce_scatter | solution.py:166
  601.4 67.6 %reduce-scatter.25.cloned.1.call-done = f32[40,1024]{1,0:T(8,128)} async-done(((f32[640,1024]{1,0:T(8,128)}), f32[40,1024]{1,0:T(8,128)}) %reduce-scatter.25.cloned.1.call-update) | async-done | bytes 163856 | tf_op jit(solution)/shard_map/reduce_scatter | solution.py:165
  669.0 61.6 %reduce-scatter.23.cloned.1.call-done = f32[40,512]{1,0:T(8,128)} async-done(((f32[640,512]{1,0:T(8,128)}), f32[40,512]{1,0:T(8,128)}) %reduce-scatter.23.cloned.1.call-update) | async-done | bytes 81936 | tf_op jit(solution)/shard_map/reduce_scatter | solution.py:166
  730.6 61.9 %reduce-scatter.19.cloned.1.call-done = f32[40,512]{1,0:T(8,128)} async-done(((f32[640,512]{1,0:T(8,128)}), f32[40,512]{1,0:T(8,128)}) %reduce-scatter.19.cloned.1.call-update) | async-done | bytes 81936 | tf_op jit(solution)/shard_map/reduce_scatter | solution.py:165
  (313 shorter events, 87.5 us)
Async XLA Ops:
  8.0 41.8 %copy-start.89 = (bf16[256]{0:T(256)(128)(2,1)S(1)}, bf16[256]{0:T(256)(128)(2,1)}, u32[]{:S(2)}) copy-start(bf16[256]{0:T(256)(128)(2,1)} %param.39) | copy-start | bytes 1540
  8.0 41.8 %copy-start.58 = (bf16[40,256]{1,0:T(8,128)(2,1)S(1)}, bf16[40,256]{1,0:T(8,128)(2,1)}, u32[]{:S(2)}) copy-start(bf16[40,256]{1,0:T(8,128)(2,1)} %param.28) | copy-start | bytes 61444
  8.0 137.8 %reduce-scatter.11.cloned.1.call-start = ((), (), s32[]{:S(2)}) async-start(), calls=%async_computation.10 | async-start | bytes 1966080 | tf_op jit(solution)/shard_map/reduce_scatter | solution.py:215
  8.1 61.7 %collective-permute-start.2 = (bf16[1,40,512]{2,1,0:T(8,128)(2,1)}, bf16[1,40,512]{2,1,0:T(8,128)(2,1)S(1)}, u32[]{:S(2)}, u32[]{:S(2)}) collective-permute-start(bf16[1,40,512]{2,1,0:T(8,128)(2,1)} %bitcast.113), channel_id=1, source_target_pairs={{0,2},{2,0},{4,6},{6,4},{8,10},{10,8},{12,14},{14,12},{16,18},{18,... | collective-permute-start | bytes 122888 | tf_op jit(solution)/shard_map/ppermute | solution.py:30
  10.3 39.5 %copy-start.61 = (f32[256]{0:T(256)}, f32[256]{0:T(256)S(1)}, u32[]{:S(2)}) copy-start(f32[256]{0:T(256)S(1)} %get-tuple-element.157) | copy-start | bytes 3076
  47.7 66.9 %collective-permute-start = (bf16[512,256]{1,0:T(8,128)(2,1)}, bf16[512,256]{1,0:T(8,128)(2,1)}, u32[]{:S(2)}, u32[]{:S(2)}) collective-permute-start(bf16[512,256]{1,0:T(8,128)(2,1)} %convolution_convert_fusion.1), channel_id=1, source_target_pairs={{0,2},{2,4},{4,6},{6,8},{8,10},{10,12},{12,14},{14,16},{16,18},{18... | collective-permute-start | bytes 786440 | tf_op jit(solution)/shard_map/ppermute | solution.py:42
  70.2 5.0 collective-permute-start.3
  74.2 34.0 %copy-start.47 = (bf16[512,128]{0,1:T(8,128)(2,1)}, bf16[512,128]{0,1:T(8,128)(2,1)S(1)}, u32[]{:S(2)}) copy-start(bf16[512,128]{0,1:T(8,128)(2,1)S(1)} %get-tuple-element.141) | copy-start | bytes 393220
  74.2 34.1 %copy-start.44 = (bf16[512,128]{0,1:T(8,128)(2,1)}, bf16[512,128]{0,1:T(8,128)(2,1)S(1)}, u32[]{:S(2)}) copy-start(bf16[512,128]{0,1:T(8,128)(2,1)S(1)} %get-tuple-element.140) | copy-start | bytes 393220
  75.3 5.9 collective-permute-start.4
  76.1 34.9 %collective-permute-start.1 = (bf16[512,256]{0,1:T(8,128)(2,1)}, bf16[512,256]{0,1:T(8,128)(2,1)}, u32[]{:S(2)}, u32[]{:S(2)}) collective-permute-start(bf16[512,256]{0,1:T(8,128)(2,1)} %pad_maximum_fusion.9), channel_id=1, source_target_pairs={{0,2},{2,4},{4,6},{6,8},{8,10},{10,12},{12,14},{14,16},{16,18},{18... | collective-permute-start | bytes 786440 | tf_op jit(solution)/shard_map/ppermute | solution.py:42
  81.3 26.9 %collective-permute-start.5 = (bf16[8,40,512]{2,1,0:T(8,128)(2,1)S(1)}, bf16[8,40,512]{2,1,0:T(8,128)(2,1)S(1)}, u32[]{:S(2)}, u32[]{:S(2)}) collective-permute-start(bf16[8,40,512]{2,1,0:T(8,128)(2,1)S(1)} %pad_maximum_fusion.8), channel_id=1, source_target_pairs={{0,16},{2,18},{4,20},{6,22},{8,24},{10,26},{12,28},{14,30},{16,0},... | collective-permute-start | bytes 983048 | tf_op jit(solution)/shard_map/ppermute | solution.py:30
  120.7 43.1 %all-gather.4.cloned.1.call-start = ((), (), s32[]{:S(2)}) async-start(), calls=%async_computation.11 | async-start | bytes 1392640 | tf_op jit(solution)/shard_map/all_gather | solution.py:158
  121.3 82.3 %all-gather.6.cloned.1.call-start = ((), (), s32[]{:S(2)}) async-start(), calls=%async_computation.12 | async-start | bytes 1392640 | tf_op jit(solution)/shard_map/all_gather | solution.py:159
  121.9 121.5 %all-gather.8.cloned.1.call-start = ((), (), s32[]{:S(2)}) async-start(), calls=%async_computation.13 | async-start | bytes 1392640 | tf_op jit(solution)/shard_map/all_gather | solution.py:160
  122.5 147.0 %reduce-scatter.13.cloned.1.call-start = ((), (), s32[]{:S(2)}) async-start(), calls=%async_computation.14 | async-start | bytes 1966080 | tf_op jit(solution)/shard_map/reduce_scatter | solution.py:229
  247.2 69.4 %reduce-scatter.15.cloned.1.call-start = ((), (), s32[]{:S(2)}) async-start(), calls=%async_computation.15 | async-start | bytes 1966080 | tf_op jit(solution)/shard_map/reduce_scatter | solution.py:250
  293.1 86.8 %all-reduce.4.cloned.1.call-start = ((), (), s32[]{:S(2)}) async-start(), calls=%async_computation.17 | async-start | bytes 1048576 | tf_op jit(solution)/shard_map/psum | solution.py:307
  335.8 4.7 collective-permute-start.6
  341.4 62.7 %reduce-scatter.17.cloned.1.call-start = ((), (), s32[]{:S(2)}) async-start(), calls=%async_computation.16 | async-start | bytes 1966080 | tf_op jit(solution)/shard_map/reduce_scatter | solution.py:319
  345.5 120.7 %reduce-scatter.21.cloned.1.call-start = ((), (), s32[]{:S(2)}) async-start(), calls=%async_computation.19 | async-start | bytes 1392640 | tf_op jit(solution)/shard_map/reduce_scatter | solution.py:167
  349.4 32.7 %copy-start.75 = (f32[256]{0:T(256)S(1)}, f32[256]{0:T(256)}, u32[]{:S(2)}) copy-start(f32[256]{0:T(256)} %copy-done.74) | copy-start | bytes 3076
  349.5 32.8 %copy-start.57 = (f32[512]{0:T(512)S(1)}, f32[512]{0:T(512)}, u32[]{:S(2)}) copy-start(f32[512]{0:T(512)} %copy-done.56) | copy-start | bytes 6148
  349.5 32.8 %copy-start.76 = (f32[512]{0:T(512)S(1)}, f32[512]{0:T(512)}, u32[]{:S(2)}) copy-start(f32[512]{0:T(512)} %get-tuple-element.154) | copy-start | bytes 6148
  349.5 9.2 %collective-permute-start.7 = (f32[512,256]{0,1:T(8,128)S(1)}, f32[512,256]{0,1:T(8,128)S(1)}, u32[]{:S(2)}, u32[]{:S(2)}) collective-permute-start(f32[512,256]{0,1:T(8,128)S(1)} %slice.103), channel_id=1, source_target_pairs={{2,0},{4,2},{6,4},{8,6},{10,8},{12,10},{14,12},{16,14},{18,16},{20... | collective-permute-start | bytes 1572872 | tf_op jit(solution)/shard_map/ppermute | solution.py:42
  384.8 149.1 %reduce-scatter.29.cloned.1.call-start = ((), (), s32[]{:S(2)}) async-start(), calls=%async_computation.23 | async-start | bytes 2785280 | tf_op jit(solution)/shard_map/reduce_scatter | solution.py:167
  388.4 213.0 %reduce-scatter.27.cloned.1.call-start = ((), (), s32[]{:S(2)}) async-start(), calls=%async_computation.22 | async-start | bytes 2785280 | tf_op jit(solution)/shard_map/reduce_scatter | solution.py:166
  392.0 277.0 %reduce-scatter.25.cloned.1.call-start = ((), (), s32[]{:S(2)}) async-start(), calls=%async_computation.21 | async-start | bytes 2785280 | tf_op jit(solution)/shard_map/reduce_scatter | solution.py:165
  395.7 334.9 %reduce-scatter.23.cloned.1.call-start = ((), (), s32[]{:S(2)}) async-start(), calls=%async_computation.20 | async-start | bytes 1392640 | tf_op jit(solution)/shard_map/reduce_scatter | solution.py:166
  398.6 393.9 %reduce-scatter.19.cloned.1.call-start = ((), (), s32[]{:S(2)}) async-start(), calls=%async_computation.18 | async-start | bytes 1392640 | tf_op jit(solution)/shard_map/reduce_scatter | solution.py:165
  401.3 50.6 %copy-start.4 = (f32[256,640]{1,0:T(8,128)S(1)}, f32[256,640]{1,0:T(8,128)}, u32[]{:S(2)}) copy-start(f32[256,640]{1,0:T(8,128)} %copy-done.3) | copy-start | bytes 1966084
  401.3 50.6 %copy-start.78 = (f32[256]{0:T(256)S(1)}, f32[256]{0:T(256)}, u32[]{:S(2)}) copy-start(f32[256]{0:T(256)} %get-tuple-element.156) | copy-start | bytes 3076
  (84 other events, 520.2 us)
Sparse Core Ops, SparseCore 0:
  120.8 24.9 reduce-scatter.10
  247.3 22.1 reduce-scatter.12
  293.2 23.2 reduce-scatter.14
  341.5 38.2 all-reduce.3
  382.0 22.1 reduce-scatter.16
  407.6 58.5 reduce-scatter.20
  470.6 63.2 reduce-scatter.28
  538.2 63.1 reduce-scatter.26
  605.8 63.1 reduce-scatter.24
  673.1 57.5 reduce-scatter.22
  734.8 57.6 reduce-scatter.18
Sparse Core Ops, SparseCore 1:
  123.5 40.3 all-gather.3
  166.0 37.6 all-gather.5
  205.8 37.6 all-gather.7
